TPU v7x, 256 devices: a whole 4x4x8 slice. The times are simulated.
256 devices in a mesh: req: 64 (over z, x, core), tp: 4 (over y).
Axes of the slice: x: 4, y: 4, z: 8, core: 2. Of those that a mesh axis runs over, the one named last changes fastest.
Arguments:
- hidden: bfloat16 [2048, 5120], P('req', 'tp'), may hold values from -8 to 8
- gain: float32 [5120], replicated, may hold values from 0.5 to 1.5
- head_weight: bfloat16 [5120, 131072], P(None, ('req', 'tp')), may hold values from -0.3 to 0.3
- token_ids: int32 [2048], P('req'), may hold values from 0 to 131071
- lengths: int32 [64], P('req'), may hold values from 1 to 32, as said below
- owner_device: int32 [64], replicated, may hold values from 0 to 63, each once
Outputs:
- logprob: float32 [2048], P('req')
- entropy: float32 [2048], P('req')
Inputs may be any that keep to these rules, and one draw needn't show every extreme that they name: `lengths`: each sequence has 1 to 32 live slots; some sequence has exactly 32. `owner_device`: A permutation of the req indices.
All inputs are finite; a program needn't handle non-finite values.
Results may differ from a plain program's by a relative error of at most 0.0041.
Values may be sent and summed in bfloat16 or wider, within the bound.
No kernel may reach another device: no remote copies, remote signals or barrier semaphores. Data moves between devices by JAX's collectives and lax.ppermute only.
A program may use at most 128 MiB of HBM per device.

v0:
```python
import math
import jax
import jax.numpy as jnp
from jax import lax
from jax.sharding import PartitionSpec as P


def finalize(peak_logit, exp_total, exp_spread, pick_logit):
    log_total = peak_logit + jnp.log(exp_total)
    return (pick_logit - log_total, log_total - exp_spread / exp_total)


def score_rows(all_rows, all_ids, columns, vocab_base):
    row_total = all_rows.shape[0]
    block_rows = math.gcd(row_total, 256)
    row_blocks = all_rows.reshape(row_total // block_rows, block_rows, all_rows.shape[1])
    id_blocks = all_ids.reshape(row_total // block_rows, block_rows)

    def score_block(block_args):
        piece_rows, piece_ids = block_args
        logits = jnp.dot(piece_rows, columns, preferred_element_type=jnp.float32)
        peak_logit = jnp.max(logits, axis=-1)
        weights_exp = jnp.exp(logits - peak_logit[:, None])
        exp_total = jnp.sum(weights_exp, axis=-1)
        exp_spread = jnp.sum(weights_exp * logits, axis=-1)
        vocab_index = vocab_base + lax.broadcasted_iota(jnp.int32, logits.shape, 1)
        pick_logit = jnp.sum(jnp.where(piece_ids[:, None] == vocab_index, logits, 0.0), axis=-1)
        return (peak_logit, exp_total, exp_spread, pick_logit)

    stats = lax.map(score_block, (row_blocks, id_blocks))
    return tuple((member.reshape(-1) for member in stats))


def local(hidden, gain, head_weight, token_ids, lengths, owner_device):
    gathered = lax.all_gather(hidden, "tp", axis=1, tiled=True)
    values = gathered.astype(jnp.float32)
    mean_square = jnp.mean(values * values, axis=-1, keepdims=True)
    normed = (values * lax.rsqrt(mean_square + 1e-05) * gain).astype(jnp.bfloat16)
    seq_slots = normed.shape[0]
    tp_count = lax.axis_size("tp")
    req_count = lax.axis_size("req")
    vocab_base = (lax.axis_index("req") * tp_count + lax.axis_index("tp")) * head_weight.shape[1]
    all_rows, all_ids = (
        lax.all_gather(normed, "req", axis=0, tiled=True),
        lax.all_gather(token_ids, "req", axis=0, tiled=True),
    )
    stats = score_rows(all_rows, all_ids, head_weight, vocab_base)
    global_peak = lax.pmax(stats[0], ("req", "tp"))
    rescale = jnp.exp(stats[0] - global_peak)
    exp_total, exp_spread, pick_logit = lax.psum(
        (stats[1] * rescale, stats[2] * rescale, stats[3]), ("req", "tp")
    )
    stats = (global_peak, exp_total, exp_spread, pick_logit)
    row_logprob, row_entropy = finalize(*stats)
    row_logprob = row_logprob.reshape(req_count, seq_slots)
    row_entropy = row_entropy.reshape(req_count, seq_slots)
    worker = owner_device[lax.axis_index("req")]
    own_logprob = lax.dynamic_index_in_dim(row_logprob, worker, 0, keepdims=False)
    own_entropy = lax.dynamic_index_in_dim(row_entropy, worker, 0, keepdims=False)
    live_mask = jnp.arange(seq_slots, dtype=jnp.int32) < lengths[0]
    return (jnp.where(live_mask, own_logprob, 0.0), jnp.where(live_mask, own_entropy, 0.0))


def solution(mesh):
    placed = (P("req", "tp"), P(), P(None, ("req", "tp")), P("req"), P("req"), P())
    return jax.shard_map(
        local, mesh=mesh, in_specs=placed, out_specs=(P("req"), P("req")), check_vma=False
    )
```

profile of v0, /device:TPU:1, one launch (start us, length us, event | category | flops | bytes accessed | tf_op | source)
XLA Modules:
  0.0 335.5 jit_solution(15491374336734146777)
XLA Ops:
  7.2 0.0 all-gather.2.cloned.1.call-start
  7.2 11.9 %all_gather.9 = bf16[32,5120]{1,0:T(8,128)(2,1)S(1)} all-gather(bf16[32,1280]{1,0:T(8,128)(2,1)} %param.8), channel_id=1, replica_groups=mesh['req'=64,'tp'=4] {'tp'}, dimensions={1}, use_global_device_ids=true | all-gather | bytes 409600 | tf_op jit(solution)/shard_map/all_gather | solution.py:35
  19.1 0.2 fusion.5
  19.3 1.6 fusion.7
  20.9 0.0 all-gather.2.cloned.1.call-update
  21.0 1.3 dynamic_slice.18
  23.5 1.3 dynamic-slice
  25.4 0.9 dynamic-update-slice
  26.3 22.6 %all-reduce = s32[2048]{0:T(1024)S(1)} all-reduce(s32[2048]{0:T(1024)S(1)} %dynamic-update-slice), channel_id=1, replica_groups=mesh['req'=64,'tp'=4] {'req'}, use_global_device_ids=true, to_apply=%add | all-reduce | flops 2048 | bytes 16384
  50.2 85.8 %all-gather.2.cloned.1.call-done = bf16[2048,5120]{1,0:T(8,128)(2,1)} async-done(((bf16[32,5120]{1,0:T(8,128)(2,1)}), bf16[2048,5120]{1,0:T(8,128)(2,1)}) %all-gather.2.cloned.1.call-update) | async-done | bytes 20971536 | tf_op jit(solution)/shard_map/all_gather | solution.py:44
  136.0 43.6 %while.16 = (s32[]{:T(128)}, f32[8,256]{1,0:T(8,128)S(1)}, f32[8,256]{1,0:T(8,128)S(1)}, f32[8,256]{1,0:T(8,128)S(1)}, f32[8,256]{1,0:T(8,128)S(1)}, /*index=5*/...) while((s32[]{:T(128)}, f32[8,256]{1,0:T(8,128)S(1)}, ...), condition=%wide.region_6.7_spmd, body=%wide.region_1.6_spmd.sunk | while | flops 1343225344 | bytes 8934021 | solution.py:30
  136.0 4.9 %fusion.16 = (f32[256]{0:T(256)S(1)}, f32[256,512]{1,0:T(8,128)S(1)}) fusion(bf16[5120,512]{1,0:T(8,128)(2,1)} %get-tuple-element.181, bf16[8,256,5120]{2,1,0:T(8,128)(2,1)} %get-tuple-element.180, s32[]{:T(128)} %get-tuple-element.164), kind=kOutput, calls=%fused_computation.24.clone.1 | convolution fusion | flops 1342308096 | bytes 8390144 | tf_op jit(solution)/shard_map/while/body/eval_jaxpr/dot_general | solution.py:21
  140.9 0.3 multiply_reduce_fusion.2
  141.5 4.9 %fusion.16 = (f32[256]{0:T(256)S(1)}, f32[256,512]{1,0:T(8,128)S(1)}) fusion(bf16[5120,512]{1,0:T(8,128)(2,1)} %get-tuple-element.181, bf16[8,256,5120]{2,1,0:T(8,128)(2,1)} %get-tuple-element.180, s32[]{:T(128)} %get-tuple-element.164), kind=kOutput, calls=%fused_computation.24.clone.1 | convolution fusion | flops 1342308096 | bytes 8390144 | tf_op jit(solution)/shard_map/while/body/eval_jaxpr/dot_general | solution.py:21
  146.4 0.3 multiply_reduce_fusion.2
  146.9 4.9 %fusion.16 = (f32[256]{0:T(256)S(1)}, f32[256,512]{1,0:T(8,128)S(1)}) fusion(bf16[5120,512]{1,0:T(8,128)(2,1)} %get-tuple-element.181, bf16[8,256,5120]{2,1,0:T(8,128)(2,1)} %get-tuple-element.180, s32[]{:T(128)} %get-tuple-element.164), kind=kOutput, calls=%fused_computation.24.clone.1 | convolution fusion | flops 1342308096 | bytes 8390144 | tf_op jit(solution)/shard_map/while/body/eval_jaxpr/dot_general | solution.py:21
  151.8 0.3 multiply_reduce_fusion.2
  152.4 4.9 %fusion.16 = (f32[256]{0:T(256)S(1)}, f32[256,512]{1,0:T(8,128)S(1)}) fusion(bf16[5120,512]{1,0:T(8,128)(2,1)} %get-tuple-element.181, bf16[8,256,5120]{2,1,0:T(8,128)(2,1)} %get-tuple-element.180, s32[]{:T(128)} %get-tuple-element.164), kind=kOutput, calls=%fused_computation.24.clone.1 | convolution fusion | flops 1342308096 | bytes 8390144 | tf_op jit(solution)/shard_map/while/body/eval_jaxpr/dot_general | solution.py:21
  157.3 0.3 multiply_reduce_fusion.2
  157.8 4.9 %fusion.16 = (f32[256]{0:T(256)S(1)}, f32[256,512]{1,0:T(8,128)S(1)}) fusion(bf16[5120,512]{1,0:T(8,128)(2,1)} %get-tuple-element.181, bf16[8,256,5120]{2,1,0:T(8,128)(2,1)} %get-tuple-element.180, s32[]{:T(128)} %get-tuple-element.164), kind=kOutput, calls=%fused_computation.24.clone.1 | convolution fusion | flops 1342308096 | bytes 8390144 | tf_op jit(solution)/shard_map/while/body/eval_jaxpr/dot_general | solution.py:21
  162.7 0.3 multiply_reduce_fusion.2
  163.3 4.9 %fusion.16 = (f32[256]{0:T(256)S(1)}, f32[256,512]{1,0:T(8,128)S(1)}) fusion(bf16[5120,512]{1,0:T(8,128)(2,1)} %get-tuple-element.181, bf16[8,256,5120]{2,1,0:T(8,128)(2,1)} %get-tuple-element.180, s32[]{:T(128)} %get-tuple-element.164), kind=kOutput, calls=%fused_computation.24.clone.1 | convolution fusion | flops 1342308096 | bytes 8390144 | tf_op jit(solution)/shard_map/while/body/eval_jaxpr/dot_general | solution.py:21
  168.2 0.3 multiply_reduce_fusion.2
  168.7 4.9 %fusion.16 = (f32[256]{0:T(256)S(1)}, f32[256,512]{1,0:T(8,128)S(1)}) fusion(bf16[5120,512]{1,0:T(8,128)(2,1)} %get-tuple-element.181, bf16[8,256,5120]{2,1,0:T(8,128)(2,1)} %get-tuple-element.180, s32[]{:T(128)} %get-tuple-element.164), kind=kOutput, calls=%fused_computation.24.clone.1 | convolution fusion | flops 1342308096 | bytes 8390144 | tf_op jit(solution)/shard_map/while/body/eval_jaxpr/dot_general | solution.py:21
  173.6 0.3 multiply_reduce_fusion.2
  174.2 4.9 %fusion.16 = (f32[256]{0:T(256)S(1)}, f32[256,512]{1,0:T(8,128)S(1)}) fusion(bf16[5120,512]{1,0:T(8,128)(2,1)} %get-tuple-element.181, bf16[8,256,5120]{2,1,0:T(8,128)(2,1)} %get-tuple-element.180, s32[]{:T(128)} %get-tuple-element.164), kind=kOutput, calls=%fused_computation.24.clone.1 | convolution fusion | flops 1342308096 | bytes 8390144 | tf_op jit(solution)/shard_map/while/body/eval_jaxpr/dot_general | solution.py:21
  179.1 0.3 multiply_reduce_fusion.2
  179.7 74.6 %pmax.7 = f32[2048]{0:T(1024)S(1)} all-reduce(f32[2048]{0:T(1024)S(1)} %bitcast.47), channel_id=1, replica_groups=mesh['req'=64,'tp'=4] {'req','tp'}, use_global_device_ids=true, to_apply=%region_8.9 | all-reduce | flops 2048 | bytes 16384 | tf_op jit(solution)/shard_map/pmax | solution.py:48
  254.3 73.7 %all-reduce.1 = (f32[2048]{0:T(1024)S(1)}, f32[2048]{0:T(1024)S(1)}, f32[2048]{0:T(1024)S(1)}) all-reduce(f32[2048]{0:T(1024)S(1)} %bitcast.49, f32[2048]{0:T(1024)S(1)} %get-tuple-element.85, f32[2048]{0:T(1024)S(1)} %get-tuple-element.84), channel_id=1, replica_groups=mesh['req'=64,'tp'=4] {'req','tp'}, use_global_device_ids=true, to_apply=%region_7.8 | all-reduce | flops 6144 | bytes 49152 | tf_op jit(solution)/shard_map/psum | solution.py:50
  328.0 0.1 reshape.45
  328.1 0.1 reshape.47
  328.1 0.5 compare_select_fusion
  (61 shorter events, 1.5 us)
Async XLA Ops:
  7.2 128.8 %all-gather.2.cloned.1.call-start = ((), (), s32[]{:S(2)}) async-start(), calls=%async_computation | async-start | bytes 21299200 | tf_op jit(solution)/shard_map/all_gather | solution.py:44
Sparse Core Ops, SparseCore 0:
  21.0 114.9 all-gather.1
where the time goes:
time: 336 us; the launch traced here: 335 us
  blocking collectives  183 us (54%)
  waiting for transfers between devices  85.8 us (26%)
  matrix products  39 us (12%)
  between operations  17.3 us (5%)
  other arithmetic  5.12 us (2%)
  local copies, waits for them, and re-layouts  4.96 us (1%)
    all_gather x1, waiting for transfers between devices, local(): lax.all_gather(normed, 'req', axis=0, tiled=True)  85.8 us
    pmax x1, blocking collectives, local(): global_peak = lax.pmax(stats[0], ('req', 'tp'))  74.6 us
    psum x1, blocking collectives, local(): lax.psum((stats[1] * rescale, stats[2] * rescale, stats[3]), ('req', 'tp'))  73.7 us
    dot_general x8, matrix products, score_block(): logits = jnp.dot(piece_rows, columns, preferred_element_type=jnp.float32)  39 us
    unnamed x1, blocking collectives  22.6 us
    all_gather x1, blocking collectives, local(): gathered = lax.all_gather(hidden, 'tp', axis=1, tiled=True)  11.9 us
  transfers between devices with their start and end apart: 1, of which 1 were waited for; matrix products, arithmetic and copies ran while one was open for 1% of the time, Pallas kernels for 0%

commit v1 on v0

--- a/solution.py
+++ b/solution.py
@@ -41,7 +41,9 @@
     req_count = lax.axis_size("req")
     vocab_base = (lax.axis_index("req") * tp_count + lax.axis_index("tp")) * head_weight.shape[1]
     all_rows, all_ids = (
-        lax.all_gather(normed, "req", axis=0, tiled=True),
+        jnp.concatenate(
+            lax.all_to_all(jnp.stack([normed] * lax.axis_size("req")), "req", 0, 0), axis=0
+        ),
         lax.all_gather(token_ids, "req", axis=0, tiled=True),
     )
     stats = score_rows(all_rows, all_ids, head_weight, vocab_base)

time: 336 us -> 701 us (2.09)
  blocking collectives: 183 us -> 628 us
  waiting for transfers between devices: 85.8 us -> 0.01 us
  starting transfers between devices: 0.04 us -> 14.5 us
  between operations: 17.3 us -> 4.1 us
    unnamed x1, blocking collectives: 22.6 us -> 463 us
    all_gather x1 -> x0, waiting for transfers between devices: 85.8 us -> none  [local(): lax.all_gather(normed, 'req', axis=0, tiled=True)]
    all_to_all x0 -> x1, starting transfers between devices: none -> 14.5 us  [local(): lax.all_to_all(jnp.stack([normed] * lax.axis_size('req')), 'req', 0, 0)]
    another operation x0 -> x1, local copies, waits for them, and re-layouts: none -> 7.4 us  [local(): jnp.stack([normed] * lax.axis_size('req'))]
  transfers between devices with their start and end apart: 1 -> 1, of which waited for: 1 -> 0; matrix products, arithmetic and copies ran while one was open for 1% -> 0% of each run, Pallas kernels for 0% -> 0%
where the time goes in v1:
time: 701 us
  blocking collectives  628 us (90%)
  matrix products  39 us (6%)
  starting transfers between devices  14.5 us (2%)
  local copies, waits for them, and re-layouts  10.5 us (1%)
    unnamed x1, blocking collectives  463 us
    pmax x1, blocking collectives, local(): global_peak = lax.pmax(stats[0], ('req', 'tp'))  78.8 us
    psum x1, blocking collectives, local(): lax.psum((stats[1] * rescale, stats[2] * rescale, stats[3]), ('req', 'tp'))  73.9 us
    dot_general x8, matrix products, score_block(): logits = jnp.dot(piece_rows, columns, preferred_element_type=jnp.float32)  39 us
    all_to_all x1, starting transfers between devices, local(): lax.all_to_all(jnp.stack([normed] * lax.axis_size('req')), 'req', 0, 0)  14.5 us
  transfers between devices with their start and end apart: 1, of which 0 were waited for; matrix products, arithmetic and copies ran while one was open for 0% of the time, Pallas kernels for 0%

profile of v1, /device:TPU:1, one launch (start us, length us, event | category | flops | bytes accessed | tf_op | source)
XLA Modules:
  0.0 700.8 jit_solution(14837446633777553902)
XLA Ops:
  0.6 11.9 %all_gather.6 = bf16[32,5120]{1,0:T(8,128)(2,1)S(1)} all-gather(bf16[32,1280]{1,0:T(8,128)(2,1)} %param.8), channel_id=1, replica_groups=mesh['req'=64,'tp'=4] {'tp'}, dimensions={1}, use_global_device_ids=true | all-gather | bytes 409600 | tf_op jit(solution)/shard_map/all_gather | solution.py:35
  12.5 0.2 fusion.5
  12.7 0.9 fusion.7
  13.6 7.4 %stack.2 = bf16[64,32,5120]{2,1,0:T(8,128)(2,1)} broadcast(bf16[32,5120]{1,0:T(8,128)(2,1)S(1)} %fusion.7), dimensions={1,2} | broadcast | bytes 21299200 | tf_op jit(solution)/shard_map/stack | solution.py:45
  21.0 14.5 %all-to-all-start = ((bf16[64,32,5120]{2,1,0:T(8,128)(2,1)}), bf16[64,32,5120]{2,1,0:T(8,128)(2,1)}, u32[]{:S(2)}, u32[]{:S(2)}) async-start(bf16[64,32,5120]{2,1,0:T(8,128)(2,1)} %stack.2), calls=%async_computation | async-start | bytes 41943040 | tf_op jit(solution)/shard_map/all_to_all | solution.py:45
  35.6 0.6 dynamic_slice.18
  37.6 0.6 dynamic-slice
  38.8 0.3 dynamic-update-slice
  39.1 463.3 %all-reduce = s32[2048]{0:T(1024)S(1)} all-reduce(s32[2048]{0:T(1024)S(1)} %dynamic-update-slice), channel_id=1, replica_groups=mesh['req'=64,'tp'=4] {'req'}, use_global_device_ids=true, to_apply=%add | all-reduce | flops 2048 | bytes 16384
  503.8 0.0 all-to-all-done
  503.8 43.6 %while.16 = (s32[]{:T(128)}, f32[8,256]{1,0:T(8,128)S(1)}, f32[8,256]{1,0:T(8,128)S(1)}, f32[8,256]{1,0:T(8,128)S(1)}, f32[8,256]{1,0:T(8,128)S(1)}, /*index=5*/...) while((s32[]{:T(128)}, f32[8,256]{1,0:T(8,128)S(1)}, ...), condition=%wide.region_6.7_spmd, body=%wide.region_1.6_spmd.sunk | while | flops 1343225344 | bytes 8934021 | solution.py:30
  503.8 4.9 fusion.16
  508.7 0.3 multiply_reduce_fusion.2
  509.2 4.9 fusion.16
  514.1 0.3 multiply_reduce_fusion.2
  514.7 4.9 fusion.16
  519.6 0.3 multiply_reduce_fusion.2
  520.1 4.9 fusion.16
  525.1 0.3 multiply_reduce_fusion.2
  525.6 4.9 fusion.16
  530.5 0.3 multiply_reduce_fusion.2
  531.1 4.9 fusion.16
  536.0 0.3 multiply_reduce_fusion.2
  536.5 4.9 fusion.16
  541.4 0.3 multiply_reduce_fusion.2
  542.0 4.9 fusion.16
  546.9 0.3 multiply_reduce_fusion.2
  547.4 78.8 %pmax.7 = f32[2048]{0:T(1024)S(1)} all-reduce(f32[2048]{0:T(1024)S(1)} %bitcast.47), channel_id=1, replica_groups=mesh['req'=64,'tp'=4] {'req','tp'}, use_global_device_ids=true, to_apply=%region_8.9 | all-reduce | flops 2048 | bytes 16384 | tf_op jit(solution)/shard_map/pmax | solution.py:50
  626.3 73.9 %all-reduce.1 = (f32[2048]{0:T(1024)S(1)}, f32[2048]{0:T(1024)S(1)}, f32[2048]{0:T(1024)S(1)}) all-reduce(f32[2048]{0:T(1024)S(1)} %bitcast.49, f32[2048]{0:T(1024)S(1)} %get-tuple-element.85, f32[2048]{0:T(1024)S(1)} %get-tuple-element.84), channel_id=1, replica_groups=mesh['req'=64,'tp'=4] {'req','tp'}, use_global_device_ids=true, to_apply=%region_7.8 | all-reduce | flops 6144 | bytes 49152 | tf_op jit(solution)/shard_map/psum | solution.py:52
  700.2 0.1 reshape.43
  700.2 0.1 reshape.45
  700.3 0.5 compare_select_fusion
  (67 shorter events, 1.5 us)
Async XLA Ops:
  21.0 14.6 %copy-start = (s32[64]{0:T(128)S(1)}, s32[64]{0:T(128)}, u32[]{:S(2)}) copy-start(s32[64]{0:T(128)} %param.13) | copy-start | bytes 772
  21.0 16.6 %copy-start.2 = (u32[256]{0:T(256)S(1)}, u32[256]{0:T(256)}, u32[]{:S(2)}) copy-start(u32[256]{0:T(256)} %constant.54) | copy-start | bytes 3076
  21.0 17.8 %copy-start.1 = (s32[32]{0:T(128)S(1)}, s32[32]{0:T(128)}, u32[]{:S(2)}) copy-start(s32[32]{0:T(128)} %param.11) | copy-start | bytes 388
  21.0 482.8 %all-to-all-start = ((bf16[64,32,5120]{2,1,0:T(8,128)(2,1)}), bf16[64,32,5120]{2,1,0:T(8,128)(2,1)}, u32[]{:S(2)}, u32[]{:S(2)}) async-start(bf16[64,32,5120]{2,1,0:T(8,128)(2,1)} %stack.2), calls=%async_computation | async-start | bytes 41943040 | tf_op jit(solution)/shard_map/all_to_all | solution.py:45
